TPU v7x, 32 devices: a whole 2x2x4 slice. The times are simulated.
32 devices in a mesh: grp: 4 (over y, core), dev: 8 (over z, x).
Axes of the slice: x: 2, y: 2, z: 4, core: 2. Of those that a mesh axis runs over, the one named last changes fastest.
Arguments:
- train_grads: bfloat16 [4096, 1024], P(('grp', 'dev')), may hold values from -192 to 192, as said below
- queries: bfloat16 [512, 1024], P('grp'), may hold values from -6 to 6
Outputs:
- scores: bfloat16 [4096, 512], P(('grp', 'dev'))
Inputs may be any that keep to these rules, and one draw needn't show every extreme that they name: `train_grads`: Real-valued projected gradients whose columns and rows differ in scale.
All inputs are finite; a program needn't handle non-finite values. Where the computation divides by a largest or mean magnitude, that divisor is 1e-20 or more.
Results may differ from a plain program's by a relative error of at most 0.001.
The roundings to bfloat16 on the way count: a program that leaves them out, or rounds other values in their place, can miss the bound.
Values may be sent and summed in bfloat16 or wider, within the bound.
No kernel may reach another device: no remote copies, remote signals or barrier semaphores. Data moves between devices by JAX's collectives and lax.ppermute only.
A program may use at most 64 MiB of HBM per device.

v0:
```python
import jax
import jax.numpy as jnp
from jax import lax
from jax.sharding import PartitionSpec as P

ITERS = 8
damping_ratio = 0.1


def local_solve(gram, own, total, width):
    normed = gram / total
    damp = damping_ratio * jnp.trace(gram) / (total * width)
    bound = jnp.max(jnp.sum(jnp.abs(normed), axis=1)) + damp
    step = 1.0 / bound
    oper = normed + damp * jnp.eye(width, dtype=jnp.float32)
    state = step * own
    for index in range(ITERS):
        state = state + step * (own - jnp.dot(state, oper, precision=lax.Precision.HIGHEST))
    return state.astype(jnp.bfloat16)


def body(train_grads, queries):
    rows, width = train_grads.shape
    ndevice = lax.axis_size("dev")
    total = rows * ndevice * lax.axis_size("grp")
    qvals = queries.astype(jnp.float32)
    qrows = qvals.shape[0] // ndevice
    qstart = lax.axis_index("dev") * qrows
    own = lax.dynamic_slice_in_dim(qvals, qstart, qrows, 0)
    gram = lax.psum(
        lax.dot_general(
            train_grads, train_grads, (((0,), (0,)), ((), ())), preferred_element_type=jnp.float32
        ),
        ("grp", "dev"),
    )
    mine = local_solve(gram, own, total, width)
    prepared = lax.all_gather(mine, "dev", axis=0, tiled=True)
    return lax.dot_general(
        train_grads,
        lax.all_gather(prepared, "grp", axis=0, tiled=True),
        (((1,), (1,)), ((), ())),
        preferred_element_type=jnp.float32,
    ).astype(jnp.bfloat16)


def solution(mesh):
    return jax.shard_map(
        body,
        mesh=mesh,
        in_specs=(P(("grp", "dev"), None), P("grp", None)),
        out_specs=P(("grp", "dev"), None),
        check_vma=False,
    )
```

profile of v0, /device:TPU:0, one launch (start us, length us, event | category | flops | bytes accessed | tf_op | source)
XLA Modules:
  0.0 242.2 jit_solution(13720680544935687470)
XLA Ops:
  6.5 0.0 copy-start
  6.5 0.0 all-reduce.2.cloned.1.call-start
  6.5 0.9 copy-done
  7.5 2.7 %fusion.21 = f32[1024,1024]{1,0:T(8,128)} fusion(bf16[128,1024]{1,0:T(8,128)(2,1)S(1)} %copy-done), kind=kOutput, calls=%fused_computation.35 | convolution fusion | flops 268435456 | bytes 4456448 | tf_op jit(solution)/shard_map/dot_general | solution.py:31
  10.2 0.0 copy-start.2
  10.2 0.0 all-reduce.2.cloned.1.call-update
  10.2 0.0 all-gather.2.cloned.1.call-start
  10.3 147.6 %all-reduce.2.cloned.1.call-done = f32[1024,1024]{1,0:T(8,128)} async-done(((f32[1024,1024]{1,0:T(8,128)}), f32[1024,1024]{1,0:T(8,128)}) %all-reduce.2.cloned.1.call-update) | async-done | bytes 4194320 | tf_op jit(solution)/shard_map/psum | solution.py:30
  157.9 3.3 %select_reduce_fusion = (f32[]{:T(128)}, f32[1024]{0:T(1024)S(1)}) fusion(f32[1024,1024]{1,0:T(8,128)} %all-reduce.2.cloned.1.call-done), kind=kLoop, calls=%fused_computation.1 | loop fusion | flops 6290431 | bytes 4198404 | tf_op jit(solution)/shard_map/jit(trace)/reduce_sum | solution.py:12
  161.9 0.6 reduce_max.9
  163.2 0.0 copy-done.2
  163.2 0.0 copy-start.1
  163.2 4.6 %fusion.2 = f32[16,1024]{1,0:T(8,128)S(1)} fusion(f32[]{:T(128)S(6)} %div.15, bf16[128,1024]{1,0:T(8,128)(2,1)S(1)} %copy-done.2, s32[]{:T(128)S(6)} %select_n.9, f32[1024,1024]{1,0:T(8,128)} %all-reduce.2.cloned.1.call-done, f32[]{:T(128)S(6)} %div.14), kind=kOutput, calls=%fused_computation.15 | convolution fusion | flops 205635584 | bytes 4327936 | tf_op jit(solution)/shard_map/dot_general | solution.py:18
  167.8 0.0 copy-done.1
  167.8 2.3 fusion.4
  170.1 2.3 fusion.6
  172.3 2.3 fusion.8
  174.6 2.3 fusion.10
  176.8 2.4 %fusion.12 = f32[16,1024]{1,0:T(8,128)S(1)} fusion(f32[16,1024]{1,0:T(8,128)S(1)} %fusion.10, f32[]{:T(128)S(6)} %div.15, bf16[128,1024]{1,0:T(8,128)(2,1)S(1)} %copy-done.2, s32[]{:T(128)S(6)} %select_n.9, f32[1024,1024]{1,0:T(8,128)S(1)} %copy-done.1, f32[]{:T(128)S(6)} %div.14), kind=kOutput, calls=%fused_computation.25 | convolution fusion | flops 205586432 | bytes 4423692 | tf_op jit(solution)/shard_map/dot_general | solution.py:18
  179.3 2.3 fusion.14
  181.5 2.3 fusion.17
  183.8 32.8 %all_gather.6 = bf16[128,1024]{1,0:T(8,128)(2,1)} all-gather(bf16[16,1024]{1,0:T(8,128)(2,1)S(1)} %fusion.17), channel_id=1, replica_groups=mesh['grp'=4,'dev'=8] {'dev'}, dimensions={0}, use_global_device_ids=true | all-gather | bytes 294912 | tf_op jit(solution)/shard_map/all_gather | solution.py:37
  216.6 0.0 all-gather.2.cloned.1.call-update
  216.7 16.3 %all-gather.2.cloned.1.call-done = bf16[512,1024]{1,0:T(8,128)(2,1)} async-done(((bf16[128,1024]{1,0:T(8,128)(2,1)}), bf16[512,1024]{1,0:T(8,128)(2,1)}) %all-gather.2.cloned.1.call-update) | async-done | bytes 1048592 | tf_op jit(solution)/shard_map/all_gather | solution.py:40
  233.0 1.7 fusion
  234.6 0.8 copy.3
Async XLA Ops:
  6.5 1.0 copy-start
  6.5 151.4 %all-reduce.2.cloned.1.call-start = ((), (), s32[]{:S(2)}) async-start(), calls=%async_computation | async-start | bytes 8388608 | tf_op jit(solution)/shard_map/psum | solution.py:30
  10.2 153.0 %copy-start.2 = (bf16[128,1024]{1,0:T(8,128)(2,1)S(1)}, bf16[128,1024]{1,0:T(8,128)(2,1)}, u32[]{:S(2)}) copy-start(bf16[128,1024]{1,0:T(8,128)(2,1)} %param.3) | copy-start | bytes 786436
  10.2 222.8 %all-gather.2.cloned.1.call-start = ((), (), s32[]{:S(2)}) async-start(), calls=%async_computation.1 | async-start | bytes 1310720 | tf_op jit(solution)/shard_map/all_gather | solution.py:40
  163.2 4.6 %copy-start.1 = (f32[1024,1024]{1,0:T(8,128)S(1)}, f32[1024,1024]{1,0:T(8,128)}, u32[]{:S(2)}) copy-start(f32[1024,1024]{1,0:T(8,128)} %all-reduce.2.cloned.1.call-done) | copy-start | bytes 12582916
Sparse Core Ops, SparseCore 0:
  12.9 144.9 all-reduce.1
  216.8 16.1 all-gather.1
where the time goes:
time: 242 us
  waiting for transfers between devices  164 us (68%)
  blocking collectives  32.8 us (14%)
  matrix products  24.9 us (10%)
  between operations  14.8 us (6%)
  other arithmetic  3.94 us (2%)
    psum x1, waiting for transfers between devices, body(): lax.psum(lax.dot_general(train_grads, train_grads, (((0,), (0,)), ((), ()...  148 us
    all_gather x1, blocking collectives, body(): prepared = lax.all_gather(mine, 'dev', axis=0, tiled=True)  32.8 us
    dot_general x8, matrix products, local_solve(): jnp.dot(state, oper, precision=lax.Precision.HIGHEST)  20.5 us
    all_gather x1, waiting for transfers between devices, body(): lax.all_gather(prepared, 'grp', axis=0, tiled=True)  16.3 us
  transfers between devices with their start and end apart: 2, of which 2 were waited for; matrix products, arithmetic and copies ran while one was open for 0% of the time, Pallas kernels for 0%

commit v1 on v0

--- a/solution.py
+++ b/solution.py
@@ -5,6 +5,23 @@
 
 ITERS = 8
 damping_ratio = 0.1
+
+
+def in_order(blocks, dim):
+    blocks = jnp.moveaxis(blocks, 0, dim)
+    lengths = blocks.shape
+    return blocks.reshape(*lengths[:dim], lengths[dim] * lengths[dim + 1], *lengths[dim + 2 :])
+
+
+def doubled(value, axis):
+    size, mine = (lax.axis_size(axis), lax.axis_index(axis))
+    parts, distance = (value[None], 1)
+    while distance < size:
+        theirs = lax.ppermute(parts, axis, [(i, i ^ distance) for i in range(size)])
+        low = mine & distance == 0
+        parts = jnp.concatenate([jnp.where(low, parts, theirs), jnp.where(low, theirs, parts)])
+        distance *= 2
+    return parts
 
 
 def local_solve(gram, own, total, width):
@@ -34,7 +51,7 @@
         ("grp", "dev"),
     )
     mine = local_solve(gram, own, total, width)
-    prepared = lax.all_gather(mine, "dev", axis=0, tiled=True)
+    prepared = in_order(doubled(mine, "dev"), 0)
     return lax.dot_general(
         train_grads,
         lax.all_gather(prepared, "grp", axis=0, tiled=True),

time: 242 us -> 226 us (0.934)
  blocking collectives: 32.8 us -> 0 us
  waiting for transfers between devices: 164 us -> 177 us
  starting transfers between devices: 0.04 us -> 3.4 us
    all_gather x1 -> x0, blocking collectives: 32.8 us -> none  [body(): prepared = lax.all_gather(mine, 'dev', axis=0, tiled=True)]
    ppermute x0 -> x3, waiting for transfers between devices: none -> 13.2 us  [doubled(): theirs = lax.ppermute(parts, axis, [(i, i ^ distance) for i in range(size)])]
    ppermute x0 -> x3, starting transfers between devices: none -> 3.36 us  [doubled(): theirs = lax.ppermute(parts, axis, [(i, i ^ distance) for i in range(size)])]
  transfers between devices with their start and end apart: 2 -> 5, of which waited for: 2 -> 5; matrix products, arithmetic and copies ran while one was open for 0% -> 0% of each run, Pallas kernels for 0% -> 0%
where the time goes in v1:
time: 226 us
  waiting for transfers between devices  177 us (78%)
  matrix products  24.9 us (11%)
  between operations  14.9 us (7%)
  other arithmetic  4.73 us (2%)
  starting transfers between devices  3.4 us (2%)
    psum x1, waiting for transfers between devices, body(): lax.psum(lax.dot_general(train_grads, train_grads, (((0,), (0,)), ((), ()...  148 us
    dot_general x8, matrix products, local_solve(): jnp.dot(state, oper, precision=lax.Precision.HIGHEST)  20.5 us
    all_gather x1, waiting for transfers between devices, body(): lax.all_gather(prepared, 'grp', axis=0, tiled=True)  15.4 us
    ppermute x3, waiting for transfers between devices, doubled(): theirs = lax.ppermute(parts, axis, [(i, i ^ distance) for i in range(size)])  13.2 us
  transfers between devices with their start and end apart: 5, of which 5 were waited for; matrix products, arithmetic and copies ran while one was open for 0% of the time, Pallas kernels for 0%

profile of v1, /device:TPU:0, one launch (start us, length us, event | category | flops | bytes accessed | tf_op | source)
XLA Modules:
  0.0 226.1 jit_solution(14214115463304786477)
XLA Ops:
  6.5 0.0 copy-start
  6.5 0.0 all-reduce.2.cloned.1.call-start
  6.5 0.9 copy-done
  7.5 2.7 %fusion.22 = f32[1024,1024]{1,0:T(8,128)} fusion(bf16[128,1024]{1,0:T(8,128)(2,1)S(1)} %copy-done), kind=kOutput, calls=%fused_computation.45 | convolution fusion | flops 268435456 | bytes 4456448 | tf_op jit(solution)/shard_map/dot_general | solution.py:48
  10.2 0.0 copy-start.2
  10.2 0.0 all-reduce.2.cloned.1.call-update
  10.2 0.0 all-gather.2.cloned.1.call-start
  10.3 147.9 %all-reduce.2.cloned.1.call-done = f32[1024,1024]{1,0:T(8,128)} async-done(((f32[1024,1024]{1,0:T(8,128)}), f32[1024,1024]{1,0:T(8,128)}) %all-reduce.2.cloned.1.call-update) | async-done | bytes 4194320 | tf_op jit(solution)/shard_map/psum | solution.py:47
  158.2 3.3 %select_reduce_fusion = (f32[]{:T(128)}, f32[1024]{0:T(1024)S(1)}) fusion(f32[1024,1024]{1,0:T(8,128)} %all-reduce.2.cloned.1.call-done), kind=kLoop, calls=%fused_computation.1 | loop fusion | flops 6290431 | bytes 4198404 | tf_op jit(solution)/shard_map/jit(trace)/reduce_sum | solution.py:29
  162.1 0.6 reduce_max.9
  163.4 0.0 copy-done.2
  163.4 0.0 copy-start.1
  163.5 4.6 %fusion.2 = f32[16,1024]{1,0:T(8,128)S(1)} fusion(f32[]{:T(128)S(6)} %div.15, bf16[128,1024]{1,0:T(8,128)(2,1)S(1)} %copy-done.2, s32[]{:T(128)S(6)} %select_n.48, f32[1024,1024]{1,0:T(8,128)} %all-reduce.2.cloned.1.call-done, f32[]{:T(128)S(6)} %div.14), kind=kOutput, calls=%fused_computation.15 | convolution fusion | flops 205635584 | bytes 4327936 | tf_op jit(solution)/shard_map/dot_general | solution.py:35
  168.1 0.0 copy-done.1
  168.1 2.3 fusion.4
  170.3 2.3 fusion.6
  172.6 2.3 fusion.8
  174.8 2.3 fusion.10
  177.1 2.4 %fusion.12 = f32[16,1024]{1,0:T(8,128)S(1)} fusion(f32[16,1024]{1,0:T(8,128)S(1)} %fusion.10, f32[]{:T(128)S(6)} %div.15, bf16[128,1024]{1,0:T(8,128)(2,1)S(1)} %copy-done.2, s32[]{:T(128)S(6)} %select_n.48, f32[1024,1024]{1,0:T(8,128)S(1)} %copy-done.1, f32[]{:T(128)S(6)} %div.14), kind=kOutput, calls=%fused_computation.25 | convolution fusion | flops 205586432 | bytes 4423692 | tf_op jit(solution)/shard_map/dot_general | solution.py:35
  179.5 2.3 fusion.14
  181.8 2.3 fusion.18
  184.1 1.4 collective-permute-start
  185.5 2.6 %collective-permute-done = bf16[1,16,1024]{2,1,0:T(8,128)(2,1)S(1)} collective-permute-done((bf16[1,16,1024]{2,1,0:T(8,128)(2,1)S(1)}, bf16[1,16,1024]{2,1,0:T(8,128)(2,1)S(1)}, u32[]{:S(2)}, u32[]{:S(2)}) %collective-permute-start) | collective-permute-done | bytes 32800 | tf_op jit(solution)/shard_map/ppermute | solution.py:20
  188.1 0.8 collective-permute-start.1
  188.9 4.6 %collective-permute-done.1 = bf16[2,16,1024]{2,1,0:T(8,128)(2,1)S(1)} collective-permute-done((bf16[2,16,1024]{2,1,0:T(8,128)(2,1)S(1)}, bf16[2,16,1024]{2,1,0:T(8,128)(2,1)S(1)}, u32[]{:S(2)}, u32[]{:S(2)}) %collective-permute-start.1) | collective-permute-done | bytes 65568 | tf_op jit(solution)/shard_map/ppermute | solution.py:20
  193.6 1.1 collective-permute-start.2
  194.7 6.0 %collective-permute-done.2 = bf16[4,16,1024]{2,1,0:T(8,128)(2,1)S(1)} collective-permute-done((bf16[4,16,1024]{2,1,0:T(8,128)(2,1)S(1)}, bf16[4,16,1024]{2,1,0:T(8,128)(2,1)S(1)}, u32[]{:S(2)}, u32[]{:S(2)}) %collective-permute-start.2) | collective-permute-done | bytes 131104 | tf_op jit(solution)/shard_map/ppermute | solution.py:20
  200.7 0.7 pad_maximum_fusion
  201.4 0.0 all-gather.2.cloned.1.call-update
  201.5 15.4 %all-gather.2.cloned.1.call-done = bf16[512,1024]{1,0:T(8,128)(2,1)} async-done(((bf16[128,1024]{1,0:T(8,128)(2,1)}), bf16[512,1024]{1,0:T(8,128)(2,1)}) %all-gather.2.cloned.1.call-update) | async-done | bytes 1048592 | tf_op jit(solution)/shard_map/all_gather | solution.py:57
  216.9 1.7 fusion
  218.5 0.8 copy.3
  (5 shorter events, 0.1 us)
Async XLA Ops:
  6.5 1.0 copy-start
  6.5 151.6 %all-reduce.2.cloned.1.call-start = ((), (), s32[]{:S(2)}) async-start(), calls=%async_computation | async-start | bytes 8388608 | tf_op jit(solution)/shard_map/psum | solution.py:47
  10.2 153.3 %copy-start.2 = (bf16[128,1024]{1,0:T(8,128)(2,1)S(1)}, bf16[128,1024]{1,0:T(8,128)(2,1)}, u32[]{:S(2)}) copy-start(bf16[128,1024]{1,0:T(8,128)(2,1)} %param.3) | copy-start | bytes 786436
  10.2 206.7 %all-gather.2.cloned.1.call-start = ((), (), s32[]{:S(2)}) async-start(), calls=%async_computation.1 | async-start | bytes 1310720 | tf_op jit(solution)/shard_map/all_gather | solution.py:57
  163.4 4.6 %copy-start.1 = (f32[1024,1024]{1,0:T(8,128)S(1)}, f32[1024,1024]{1,0:T(8,128)}, u32[]{:S(2)}) copy-start(f32[1024,1024]{1,0:T(8,128)} %all-reduce.2.cloned.1.call-done) | copy-start | bytes 12582916
  184.1 4.0 %collective-permute-start = (bf16[1,16,1024]{2,1,0:T(8,128)(2,1)S(1)}, bf16[1,16,1024]{2,1,0:T(8,128)(2,1)S(1)}, u32[]{:S(2)}, u32[]{:S(2)}) collective-permute-start(bf16[1,16,1024]{2,1,0:T(8,128)(2,1)S(1)} %fusion.18), channel_id=1, source_target_pairs={{0,1},{1,0},{2,3},{3,2},{4,5},{5,4},{6,7},{7,6},{8,9},{9,8},{10,11... | collective-permute-start | bytes 98312 | tf_op jit(solution)/shard_map/ppermute | solution.py:20
  188.1 5.4 %collective-permute-start.1 = (bf16[2,16,1024]{2,1,0:T(8,128)(2,1)S(1)}, bf16[2,16,1024]{2,1,0:T(8,128)(2,1)S(1)}, u32[]{:S(2)}, u32[]{:S(2)}) collective-permute-start(bf16[2,16,1024]{2,1,0:T(8,128)(2,1)S(1)} %pad_maximum_fusion.2), channel_id=1, source_target_pairs={{0,2},{1,3},{2,0},{3,1},{4,6},{5,7},{6,4},{7,5},{8,10},{9,11},{10,... | collective-permute-start | bytes 196616 | tf_op jit(solution)/shard_map/ppermute | solution.py:20
  193.6 7.1 %collective-permute-start.2 = (bf16[4,16,1024]{2,1,0:T(8,128)(2,1)S(1)}, bf16[4,16,1024]{2,1,0:T(8,128)(2,1)S(1)}, u32[]{:S(2)}, u32[]{:S(2)}) collective-permute-start(bf16[4,16,1024]{2,1,0:T(8,128)(2,1)S(1)} %pad_maximum_fusion.1), channel_id=1, source_target_pairs={{0,4},{1,5},{2,6},{3,7},{4,0},{5,1},{6,2},{7,3},{8,12},{9,13},{10,... | collective-permute-start | bytes 393224 | tf_op jit(solution)/shard_map/ppermute | solution.py:20
Sparse Core Ops, SparseCore 0:
  12.9 145.2 all-reduce.1
  201.6 15.2 all-gather.1
